TPU v7x, 512 devices: a whole 4x8x8 slice. The times are simulated.
512 devices in a mesh: seq: 64 (over z, x, core), head: 8 (over y).
Axes of the slice: x: 4, y: 8, z: 8, core: 2. Of those that a mesh axis runs over, the one named last changes fastest.
Arguments:
- query_proj: bfloat16 [65536, 512], P(('seq', 'head')), may hold values from -4 to 4
- key_proj: bfloat16 [65536, 512], P(('seq', 'head')), may hold values from -8 to 8
- value_proj: bfloat16 [65536, 4096], P(('seq', 'head')), may hold values from -6.5 to 6.5
- conv_query: float32 [3, 512], replicated, may hold values from -1 to 1
- conv_key: float32 [3, 512], replicated, may hold values from -1 to 1
- conv_value: float32 [3, 4096], replicated, may hold values from -1 to 1
Outputs:
- mixed_out: bfloat16 [65536, 4096], P(('seq', 'head'))
All inputs are finite; a program needn't handle non-finite values.
Results may differ from a plain program's by a relative error of at most 0.0027.
Values may be sent and summed in bfloat16 or wider, within the bound.
A program may use at most 128 MiB of HBM per device.

v0:
```python
import jax
import jax.numpy as jnp
import numpy as np
from jax import lax
from jax.sharding import PartitionSpec as P

KD = 16
VD = 128
SPAN = 128
KERNEL = 3


def carried_in(part, axis, combine, identity):
    place = lax.axis_index(axis)
    gathered = jax.tree.map(lambda a: lax.all_gather(a, axis), part)
    state = jax.tree.map(lambda a, e: jnp.zeros_like(a) + jnp.asarray(e, a.dtype), part, identity)

    def one(step, state):
        return combine(
            state, jax.tree.map(lambda a: lax.dynamic_index_in_dim(a, step, 0, False), gathered)
        )

    return lax.fori_loop(0, place, one, state)


def passed_along(shard, axis, by):
    size = lax.axis_size(axis)
    pairs = [(i, i + by) for i in range(size) if 0 <= i + by < size]
    return lax.ppermute(shard, axis, pairs)


def features(values):
    scaled = values * KD ** (-0.25)
    first_index, second_index = np.triu_indices(KD, 1)
    cross = scaled[..., first_index] * scaled[..., second_index]
    return jnp.concatenate(
        [jnp.ones_like(scaled[..., :1]), scaled, scaled * scaled * 0.5**0.5, cross], axis=-1
    )


def convolve_rows(row_block, before, tap_rows):
    joined = jnp.concatenate([before, row_block], axis=0).astype(jnp.float32)
    length = row_block.shape[0]
    width = tap_rows.shape[0]
    summed = jnp.zeros((length, row_block.shape[1]), jnp.float32)
    for offset in range(width):
        start = width - 1 - offset
        summed = summed + tap_rows[offset] * joined[start : start + length]
    return summed


def combine_sums(earlier, later):
    return (earlier[0] + later[0], earlier[1] + later[1])


def carried_sums(total_state, total_norm):
    identity = (jnp.zeros_like(total_state), jnp.zeros_like(total_norm))
    return carried_in((total_state, total_norm), "seq", combine_sums, identity)


def state_terms(query_float, state_part, norm_part):
    numer_term = jnp.einsum(
        "nchf,nhfv->nchv",
        query_float,
        state_part,
        precision=lax.Precision.HIGHEST,
        preferred_element_type=jnp.float32,
    )
    denom_term = jnp.einsum(
        "nchf,nhf->nch",
        query_float,
        norm_part,
        precision=lax.Precision.HIGHEST,
        preferred_element_type=jnp.float32,
    )
    return (numer_term, denom_term)


def on_device(query_proj, key_proj, value_proj, conv_query, conv_key, conv_value):
    margin = KERNEL - 1
    query_rows, key_rows, value_rows = (
        lax.all_to_all(query_proj, "head", split_axis=1, concat_axis=0, tiled=True),
        lax.all_to_all(key_proj, "head", split_axis=1, concat_axis=0, tiled=True),
        lax.all_to_all(value_proj, "head", split_axis=1, concat_axis=0, tiled=True),
    )
    group_count = lax.axis_size("head")
    group_index = lax.axis_index("head")
    head_count = query_proj.shape[1] // KD // group_count
    taps_query = lax.dynamic_slice_in_dim(
        conv_query, group_index * head_count * KD, head_count * KD, 1
    )
    taps_key = lax.dynamic_slice_in_dim(conv_key, group_index * head_count * KD, head_count * KD, 1)
    taps_value = lax.dynamic_slice_in_dim(
        conv_value, group_index * head_count * VD, head_count * VD, 1
    )
    before = passed_along(
        (query_rows[-margin:], key_rows[-margin:], value_rows[-margin:]), "seq", 1
    )
    query_conv = convolve_rows(query_rows, before[0], taps_query)
    key_conv = convolve_rows(key_rows, before[1], taps_key)
    value_conv = convolve_rows(value_rows, before[2], taps_value).astype(jnp.bfloat16)
    length = query_conv.shape[0]
    block_count = length // SPAN
    query_feat = features(query_conv.reshape(block_count, SPAN, head_count, KD)).astype(
        jnp.bfloat16
    )
    key_feat = features(key_conv.reshape(block_count, SPAN, head_count, KD)).astype(jnp.bfloat16)
    value_block = value_conv.reshape(block_count, SPAN, head_count, VD)
    causal = jnp.arange(SPAN)[:, None] >= jnp.arange(SPAN)[None, :]
    scores = jnp.einsum("nchf,nmhf->nhcm", query_feat, key_feat, preferred_element_type=jnp.float32)
    scores = jnp.where(causal, scores, jnp.float32(0.0))
    inner_den = jnp.sum(scores, axis=-1).transpose(0, 2, 1)
    inner_num = jnp.einsum(
        "nhcm,nmhv->nchv",
        scores.astype(jnp.bfloat16),
        value_block,
        preferred_element_type=jnp.float32,
    )
    block_state = jnp.einsum(
        "nmhf,nmhv->nhfv", key_feat, value_block, preferred_element_type=jnp.float32
    )
    block_norm = jnp.sum(key_feat.astype(jnp.float32), axis=1)
    prefix_state = jnp.concatenate(
        [jnp.zeros_like(block_state[:1]), jnp.cumsum(block_state, axis=0)[:-1]], axis=0
    )
    prefix_norm = jnp.concatenate(
        [jnp.zeros_like(block_norm[:1]), jnp.cumsum(block_norm, axis=0)[:-1]], axis=0
    )
    total_state = prefix_state[-1] + block_state[-1]
    total_norm = prefix_norm[-1] + block_norm[-1]
    query_float = query_feat.astype(jnp.float32)
    numer_term, denom_term = state_terms(query_float, prefix_state, prefix_norm)
    numerator = inner_num + numer_term
    denominator = inner_den + denom_term
    device_state, device_norm = carried_sums(total_state, total_norm)
    numerator = numerator + jnp.einsum(
        "nchf,hfv->nchv",
        query_float,
        device_state,
        precision=lax.Precision.HIGHEST,
        preferred_element_type=jnp.float32,
    )
    denominator = denominator + jnp.einsum(
        "nchf,hf->nch",
        query_float,
        device_norm,
        precision=lax.Precision.HIGHEST,
        preferred_element_type=jnp.float32,
    )
    result_rows = (
        (numerator / denominator[..., None]).astype(jnp.bfloat16).reshape(length, head_count * VD)
    )
    result_rows = lax.all_to_all(result_rows, "head", split_axis=0, concat_axis=1, tiled=True)
    return result_rows


def solution(mesh):
    in_specs = (
        P(("seq", "head"), None),
        P(("seq", "head"), None),
        P(("seq", "head"), None),
        P(),
        P(),
        P(),
    )
    out_specs = P(("seq", "head"), None)
    return jax.shard_map(
        on_device, mesh=mesh, in_specs=in_specs, out_specs=out_specs, check_vma=False
    )
```

profile of v0, /device:TPU:455, one launch (start us, length us, event | category | flops | bytes accessed | tf_op | source)
XLA Modules:
  0.0 331.2 jit_solution(399916114119146279)
XLA Ops:
  6.5 1.7 copy.72
  8.2 6.8 %all-to-all-start.2 = ((bf16[128,8,64]{0,2,1:T(8,128)(2,1)}), bf16[128,8,64]{0,2,1:T(8,128)(2,1)S(1)}, u32[]{:S(2)}, u32[]{:S(2)}) async-start(bf16[128,8,64]{0,2,1:T(8,128)(2,1)} %bitcast.15), calls=%async_computation.2 | async-start | bytes 262144 | tf_op jit(solution)/shard_map/all_to_all | solution.py:83
  15.0 2.3 copy.62
  17.3 5.5 %all-to-all-done.2 = bf16[128,8,64]{0,2,1:T(8,128)(2,1)S(1)} async-done(((bf16[128,8,64]{0,2,1:T(8,128)(2,1)}), bf16[128,8,64]{0,2,1:T(8,128)(2,1)S(1)}, u32[]{:S(2)}, u32[]{:S(2)}) %all-to-all-start.2) | async-done | bytes 131104 | tf_op jit(solution)/shard_map/all_to_all | solution.py:83
  22.8 3.6 %all-to-all-start = ((bf16[128,8,512]{0,2,1:T(8,128)(2,1)}), bf16[128,8,512]{0,2,1:T(8,128)(2,1)S(1)}, u32[]{:S(2)}, u32[]{:S(2)}) async-start(bf16[128,8,512]{0,2,1:T(8,128)(2,1)} %bitcast.3), calls=%async_computation | async-start | bytes 2097152 | tf_op jit(solution)/shard_map/all_to_all | solution.py:84
  28.2 1.3 collective-permute-start.2
  29.5 3.5 %collective-permute-done.2 = bf16[2,64]{0,1:T(8,128)(2,1)S(1)} collective-permute-done((bf16[2,64]{0,1:T(8,128)(2,1)S(1)}, bf16[2,64]{0,1:T(8,128)(2,1)S(1)}, u32[]{:S(2)}, u32[]{:S(2)}) %collective-permute-start.2) | collective-permute-done | bytes 288 | tf_op jit(solution)/shard_map/ppermute | solution.py:29
  34.3 2.1 gather_fusion.3
  36.4 4.7 %fusion.16 = bf16[8,128,4,120]{1,3,2,0:T(8,128)(2,1)} fusion(f32[120,8,128,4]{2,1,3,0:T(8,128)} %gather_fusion.3, f32[120,8,128,4]{2,1,3,0:T(8,128)S(1)} %gather_fusion.2), kind=kLoop, calls=%fused_computation.35 | loop fusion | flops 983040 | bytes 4915200 | tf_op jit(solution)/shard_map/convert.3
  41.1 14.3 %all-to-all-done = bf16[128,8,512]{0,2,1:T(8,128)(2,1)S(1)} async-done(((bf16[128,8,512]{0,2,1:T(8,128)(2,1)}), bf16[128,8,512]{0,2,1:T(8,128)(2,1)S(1)}, u32[]{:S(2)}, u32[]{:S(2)}) %all-to-all-start) | async-done | bytes 1048608 | tf_op jit(solution)/shard_map/all_to_all | solution.py:84
  55.9 1.3 collective-permute-start
  57.4 1.7 collective-permute-done
  62.0 2.3 fusion.34
  66.1 3.4 %all-to-all-start.1 = ((bf16[128,8,64]{0,2,1:T(8,128)(2,1)}), bf16[128,8,64]{0,2,1:T(8,128)(2,1)S(1)}, u32[]{:S(2)}, u32[]{:S(2)}) async-start(bf16[128,8,64]{0,2,1:T(8,128)(2,1)} %bitcast.9), calls=%async_computation.1 | async-start | bytes 262144 | tf_op jit(solution)/shard_map/all_to_all | solution.py:82
  69.5 7.9 %all-to-all-done.1 = bf16[128,8,64]{0,2,1:T(8,128)(2,1)S(1)} async-done(((bf16[128,8,64]{0,2,1:T(8,128)(2,1)}), bf16[128,8,64]{0,2,1:T(8,128)(2,1)S(1)}, u32[]{:S(2)}, u32[]{:S(2)}) %all-to-all-start.1) | async-done | bytes 131104 | tf_op jit(solution)/shard_map/all_to_all | solution.py:82
  77.5 1.3 collective-permute-start.1
  78.8 4.7 %collective-permute-done.1 = bf16[2,64]{0,1:T(8,128)(2,1)S(1)} collective-permute-done((bf16[2,64]{0,1:T(8,128)(2,1)S(1)}, bf16[2,64]{0,1:T(8,128)(2,1)S(1)}, u32[]{:S(2)}, u32[]{:S(2)}) %collective-permute-start.1) | collective-permute-done | bytes 288 | tf_op jit(solution)/shard_map/ppermute | solution.py:29
  83.9 2.1 gather_fusion
  86.0 2.1 gather_fusion.1
  88.2 2.6 convert_reduce_fusion
  90.8 51.5 %all_gather.9 = f32[64,4,153]{2,1,0:T(4,128)} all-gather(f32[1,4,153]{2,1,0:T(4,128)S(1)} %slice_add_fusion.1), channel_id=1, replica_groups=mesh['seq'=64,'head'=8] {'seq'}, dimensions={0}, use_global_device_ids=true | all-gather | bytes 159120 | tf_op jit(solution)/shard_map/all_gather | solution.py:15
  142.4 3.7 %fusion.15 = bf16[8,128,4,120]{1,3,2,0:T(8,128)(2,1)S(1)} fusion(f32[120,8,128,4]{2,1,3,0:T(8,128)} %gather_fusion.1, f32[120,8,128,4]{2,1,3,0:T(8,128)S(1)} %copy-done.2), kind=kLoop, calls=%fused_computation.34 | loop fusion | flops 983040 | bytes 4915200 | tf_op jit(solution)/shard_map/convert.7
  146.7 1.1 fusion.29
  147.9 1.1 select_reduce_fusion
  149.4 1.9 fusion.12
  151.3 4.7 %fusion.1 = f32[8,4,128,128]{3,2,1,0:T(8,128)} fusion(bf16[8,128,4,153]{1,3,2,0:T(8,128)(2,1)S(1)} %pad_maximum_fusion, f32[8,4,153,128]{3,2,1,0:T(8,128)S(1)} %fusion.34), kind=kOutput, calls=%fused_computation.9 | convolution fusion | flops 842268672 | bytes 5701632 | tf_op jit(solution)/shard_map/nchf,nhfv->nchv/dot_general | solution.py:62
  156.0 16.8 %all-gather.2.cloned.1.call-done = f32[64,4,153,128]{3,1,2,0:T(4,128)} async-done(((f32[1,4,153,128]{3,1,2,0:T(4,128)}), f32[64,4,153,128]{3,1,2,0:T(4,128)}) %all-gather.2.cloned.1.call-update) | async-done | bytes 20054032 | tf_op jit(solution)/shard_map/all_gather | solution.py:15
  172.8 111.9 %while.12 = (s32[]{:T(128)}, f32[4,153,128]{2,1,0:T(8,128)S(1)}, f32[4,153]{1,0:T(4,128)S(1)}, s32[]{:T(128)}, f32[64,4,153,128]{3,1,2,0:T(4,128)}, /*index=5*/f...) while((s32[]{:T(128)}, f32[4,153,128]{2,1,0:T(8,128)S(1)}, f32[4,153]{1,0:T(4,128)S(1)}, s32[]{:T(128)}, ...), condition=%wide.region_4.5_spmd, body=%wide.region_3.4_spmd.sunk | while | flops 78953 | bytes 1574199 | solution.py:23
  172.8 1.1 constant_dynamic-slice_fusion.5
  174.7 1.0 constant_dynamic-slice_fusion.5
  176.5 1.0 constant_dynamic-slice_fusion.5
  178.3 1.0 constant_dynamic-slice_fusion.5
  180.1 1.0 constant_dynamic-slice_fusion.5
  181.8 1.0 constant_dynamic-slice_fusion.5
  183.6 1.0 constant_dynamic-slice_fusion.5
  185.4 1.0 constant_dynamic-slice_fusion.5
  187.2 1.0 constant_dynamic-slice_fusion.5
  188.9 1.0 constant_dynamic-slice_fusion.5
  190.7 1.0 constant_dynamic-slice_fusion.5
  192.5 1.0 constant_dynamic-slice_fusion.5
  194.2 1.0 constant_dynamic-slice_fusion.5
  196.0 1.0 constant_dynamic-slice_fusion.5
  197.8 1.0 constant_dynamic-slice_fusion.5
  199.6 1.0 constant_dynamic-slice_fusion.5
  201.3 1.0 constant_dynamic-slice_fusion.5
  203.1 1.0 constant_dynamic-slice_fusion.5
  204.9 1.0 constant_dynamic-slice_fusion.5
  206.6 1.0 constant_dynamic-slice_fusion.5
  208.4 1.0 constant_dynamic-slice_fusion.5
  210.2 1.0 constant_dynamic-slice_fusion.5
  212.0 1.0 constant_dynamic-slice_fusion.5
  213.7 1.0 constant_dynamic-slice_fusion.5
  215.5 1.0 constant_dynamic-slice_fusion.5
  217.3 1.0 constant_dynamic-slice_fusion.5
  219.0 1.0 constant_dynamic-slice_fusion.5
  220.8 1.0 constant_dynamic-slice_fusion.5
  222.6 1.0 constant_dynamic-slice_fusion.5
  224.4 1.0 constant_dynamic-slice_fusion.5
  226.1 1.0 constant_dynamic-slice_fusion.5
  227.9 1.0 constant_dynamic-slice_fusion.5
  252.7 1.0 constant_dynamic-slice_fusion.5
  285.3 3.5 %fusion.7 = bf16[8,128,4,128]{1,3,2,0:T(8,128)(2,1)S(1)} fusion(f32[8,4,128,128]{3,2,1,0:T(8,128)} %fusion.12, f32[8,4,128,128]{3,2,1,0:T(8,128)} %fusion.1, bf16[8,128,4,153]{1,3,2,0:T(8,128)(2,1)S(1)} %copy-done.1, f32[8,128,4]{1,2,0:T(4,128)S(1)} %bitcast_add_fusion.2, f32[4,153,128]{2,1,0:T(8,128)S(1)} %get-tuple-element.39), kind=kOutput, calls=%fused_computation.19 | convolution fusion | flops 964689920 | bytes 6825984 | tf_op jit(solution)/shard_map/nchf,hfv->nchv/dot_general | solution.py:136
  288.8 34.3 %all_to_all.76 = bf16[8,128,512]{1,2,0:T(8,128)(2,1)S(1)} all-to-all(bf16[8,128,512]{1,2,0:T(8,128)(2,1)S(1)} %bitcast.103), channel_id=1, replica_groups=mesh['seq'=64,'head'=8] {'head'}, dimensions={0} | all-to-all | bytes 2097152 | tf_op jit(solution)/shard_map/all_to_all | solution.py:153
  323.1 1.3 copy.94
  (219 shorter events, 89.0 us)
Async XLA Ops:
  8.2 14.6 %all-to-all-start.2 = ((bf16[128,8,64]{0,2,1:T(8,128)(2,1)}), bf16[128,8,64]{0,2,1:T(8,128)(2,1)S(1)}, u32[]{:S(2)}, u32[]{:S(2)}) async-start(bf16[128,8,64]{0,2,1:T(8,128)(2,1)} %bitcast.15), calls=%async_computation.2 | async-start | bytes 262144 | tf_op jit(solution)/shard_map/all_to_all | solution.py:83
  15.0 11.4 %copy-start.9 = (s32[120]{0:T(128)S(1)}, s32[120]{0:T(128)}, u32[]{:S(2)}) copy-start(s32[120]{0:T(128)} %constant.72) | copy-start | bytes 1444
  15.0 14.5 %copy-start.8 = (s32[120]{0:T(128)S(1)}, s32[120]{0:T(128)}, u32[]{:S(2)}) copy-start(s32[120]{0:T(128)} %constant.73) | copy-start | bytes 1444
  22.8 32.6 %all-to-all-start = ((bf16[128,8,512]{0,2,1:T(8,128)(2,1)}), bf16[128,8,512]{0,2,1:T(8,128)(2,1)S(1)}, u32[]{:S(2)}, u32[]{:S(2)}) async-start(bf16[128,8,512]{0,2,1:T(8,128)(2,1)} %bitcast.3), calls=%async_computation | async-start | bytes 2097152 | tf_op jit(solution)/shard_map/all_to_all | solution.py:84
  26.4 146.4 %all-gather.2.cloned.1.call-start = ((), (), s32[]{:S(2)}) async-start(), calls=%async_computation.4 | async-start | bytes 20367360 | tf_op jit(solution)/shard_map/all_gather | solution.py:15
  28.2 4.8 %collective-permute-start.2 = (bf16[2,64]{0,1:T(8,128)(2,1)S(1)}, bf16[2,64]{0,1:T(8,128)(2,1)S(1)}, u32[]{:S(2)}, u32[]{:S(2)}) collective-permute-start(bf16[2,64]{0,1:T(8,128)(2,1)S(1)} %slice.126), channel_id=1, source_target_pairs={{0,8},{8,16},{16,24},{24,32},{32,40},{40,48},{48,56},{56,64},{64,7... | collective-permute-start | bytes 776 | tf_op jit(solution)/shard_map/ppermute | solution.py:29
  55.9 3.1 collective-permute-start
  60.0 1.3 copy-start.5
  60.3 1.0 copy-start.3
  62.0 3.3 %copy-start.7 = (bf16[128,512]{1,0:T(8,128)(2,1)S(1)}, bf16[128,512]{1,0:T(8,128)(2,1)}, u32[]{:S(2)}) copy-start(bf16[128,512]{1,0:T(8,128)(2,1)} %param.16) | copy-start | bytes 393220
  66.1 11.3 %all-to-all-start.1 = ((bf16[128,8,64]{0,2,1:T(8,128)(2,1)}), bf16[128,8,64]{0,2,1:T(8,128)(2,1)S(1)}, u32[]{:S(2)}, u32[]{:S(2)}) async-start(bf16[128,8,64]{0,2,1:T(8,128)(2,1)} %bitcast.9), calls=%async_computation.1 | async-start | bytes 262144 | tf_op jit(solution)/shard_map/all_to_all | solution.py:82
  77.5 6.0 %collective-permute-start.1 = (bf16[2,64]{0,1:T(8,128)(2,1)S(1)}, bf16[2,64]{0,1:T(8,128)(2,1)S(1)}, u32[]{:S(2)}, u32[]{:S(2)}) collective-permute-start(bf16[2,64]{0,1:T(8,128)(2,1)S(1)} %slice.122), channel_id=1, source_target_pairs={{0,8},{8,16},{16,24},{24,32},{32,40},{40,48},{48,56},{56,64},{64,7... | collective-permute-start | bytes 776 | tf_op jit(solution)/shard_map/ppermute | solution.py:29
  88.1 54.3 %copy-start.2 = (f32[120,8,128,4]{2,1,3,0:T(8,128)S(1)}, f32[120,8,128,4]{2,1,3,0:T(8,128)}, u32[]{:S(2)}) copy-start(f32[120,8,128,4]{2,1,3,0:T(8,128)} %gather_fusion) | copy-start | bytes 5898244
  146.1 1.7 copy-start.6
  146.7 4.6 %copy-start = (bf16[8,128,4,153]{1,3,2,0:T(8,128)(2,1)}, bf16[8,128,4,153]{1,3,2,0:T(8,128)(2,1)S(1)}, u32[]{:S(2)}) copy-start(bf16[8,128,4,153]{1,3,2,0:T(8,128)(2,1)S(1)} %pad_maximum_fusion) | copy-start | bytes 3760132
  147.9 1.5 copy-start.4
  172.8 111.9 %copy-start.1 = (bf16[8,128,4,153]{1,3,2,0:T(8,128)(2,1)S(1)}, bf16[8,128,4,153]{1,3,2,0:T(8,128)(2,1)}, u32[]{:S(2)}) copy-start(bf16[8,128,4,153]{1,3,2,0:T(8,128)(2,1)} %copy-done) | copy-start | bytes 3760132
Sparse Core Ops, SparseCore 0:
  65.5 107.2 all-gather.1
where the time goes:
time: 336 us; the launch traced here: 331 us
  blocking collectives  85.8 us (26%)
  local copies, waits for them, and re-layouts  80.8 us (24%)
  other arithmetic  64.5 us (19%)
  waiting for transfers between devices  54.4 us (16%)
  starting transfers between devices  17.6 us (5%)
  between operations  13.8 us (4%)
  matrix products  13.6 us (4%)
    dynamic_slice x63, local copies, waits for them, and re-layouts, one(): lax.dynamic_index_in_dim(a, step, 0, False)  62.4 us
    all_gather x1, blocking collectives, carried_in(): gathered = jax.tree.map(lambda a: lax.all_gather(a, axis), part)  51.5 us
    add x126, other arithmetic, combine_sums(): return (earlier[0] + later[0], earlier[1] + later[1])  48.7 us
    all_to_all x1, blocking collectives, on_device(): lax.all_to_all(result_rows, 'head', split_axis=0, concat_axis=1, tiled=True)  34.3 us
    all_gather x1, waiting for transfers between devices, carried_in(): gathered = jax.tree.map(lambda a: lax.all_gather(a, axis), part)  16.8 us
    all_to_all x1, waiting for transfers between devices, on_device(): lax.all_to_all(value_proj, 'head', split_axis=1, concat_axis=0, tiled=True)  14.3 us
    ppermute x3, waiting for transfers between devices, passed_along(): return lax.ppermute(shard, axis, pairs)  9.88 us
    another operation x4, other arithmetic  8.56 us
  transfers between devices with their start and end apart: 7, of which 7 were waited for; matrix products, arithmetic and copies ran while one was open for 10% of the time, Pallas kernels for 0%

commit v1 on v0

--- a/solution.py
+++ b/solution.py
@@ -81,7 +81,12 @@
     query_rows, key_rows, value_rows = (
         lax.all_to_all(query_proj, "head", split_axis=1, concat_axis=0, tiled=True),
         lax.all_to_all(key_proj, "head", split_axis=1, concat_axis=0, tiled=True),
-        lax.all_to_all(value_proj, "head", split_axis=1, concat_axis=0, tiled=True),
+        jnp.concatenate(
+            lax.all_to_all(
+                jnp.stack(jnp.split(value_proj, lax.axis_size("head"), axis=1)), "head", 0, 0
+            ),
+            axis=0,
+        ),
     )
     group_count = lax.axis_size("head")
     group_index = lax.axis_index("head")

time: 336 us -> 348 us (1.036)
  local copies, waits for them, and re-layouts: 80.8 us -> 91.8 us
  waiting for transfers between devices: 54.4 us -> 50.7 us
    unnamed x25 -> x32, local copies, waits for them, and re-layouts: 6.21 us -> 15.1 us
    all_to_all x1, waiting for transfers between devices: 5.48 us -> 0.01 us  [on_device(): lax.all_to_all(key_proj, 'head', split_axis=1, concat_axis=0, tiled=True)]
  transfers between devices with their start and end apart: 7 -> 7, of which waited for: 7 -> 6; matrix products, arithmetic and copies ran while one was open for 10% -> 13% of each run, Pallas kernels for 0% -> 0%
where the time goes in v1:
time: 348 us; the launch traced here: 343 us
  local copies, waits for them, and re-layouts  91.8 us (26%)
  blocking collectives  85.5 us (25%)
  other arithmetic  65.8 us (19%)
  waiting for transfers between devices  50.7 us (15%)
  starting transfers between devices  20.7 us (6%)
  between operations  13.8 us (4%)
  matrix products  13.5 us (4%)
    dynamic_slice x63, local copies, waits for them, and re-layouts, one(): lax.dynamic_index_in_dim(a, step, 0, False)  62.4 us
    all_gather x1, blocking collectives, carried_in(): gathered = jax.tree.map(lambda a: lax.all_gather(a, axis), part)  51.2 us
    add x126, other arithmetic, combine_sums(): return (earlier[0] + later[0], earlier[1] + later[1])  48.7 us
    all_to_all x1, blocking collectives, on_device(): lax.all_to_all(result_rows, 'head', split_axis=0, concat_axis=1, tiled=True)  34.3 us
    all_gather x1, waiting for transfers between devices, carried_in(): gathered = jax.tree.map(lambda a: lax.all_gather(a, axis), part)  17.1 us
    all_to_all x1, waiting for transfers between devices, on_device(): lax.all_to_all(jnp.stack(jnp.split(value_proj, lax.axis_size('head'), axi...  16.2 us
    unnamed x32, local copies, waits for them, and re-layouts  15.1 us
    ppermute x3, waiting for transfers between devices, passed_along(): return lax.ppermute(shard, axis, pairs)  9.66 us
  transfers between devices with their start and end apart: 7, of which 6 were waited for; matrix products, arithmetic and copies ran while one was open for 13% of the time, Pallas kernels for 0%

profile of v1, /device:TPU:455, one launch (start us, length us, event | category | flops | bytes accessed | tf_op | source)
XLA Modules:
  0.0 342.6 jit_solution(7009587328763848942)
XLA Ops:
  6.5 1.7 copy.51
  8.2 6.8 %all-to-all-start.2 = ((bf16[128,8,64]{0,2,1:T(8,128)(2,1)}), bf16[128,8,64]{0,2,1:T(8,128)(2,1)S(1)}, u32[]{:S(2)}, u32[]{:S(2)}) async-start(bf16[128,8,64]{0,2,1:T(8,128)(2,1)} %bitcast.21), calls=%async_computation.2 | async-start | bytes 262144 | tf_op jit(solution)/shard_map/all_to_all | solution.py:83
  15.0 1.6 bitcast_dynamic-update-slice_fusion.7
  16.6 1.6 bitcast_dynamic-update-slice_fusion.6
  18.2 1.6 bitcast_dynamic-update-slice_fusion.5
  19.8 1.6 bitcast_dynamic-update-slice_fusion.4
  21.3 1.6 bitcast_dynamic-update-slice_fusion.3
  22.9 1.6 bitcast_dynamic-update-slice_fusion.2
  24.5 1.6 bitcast_dynamic-update-slice_fusion.1
  26.0 1.6 bitcast_dynamic-update-slice_fusion
  27.6 6.6 %all-to-all-start = ((bf16[8,128,512]{2,1,0:T(8,128)(2,1)}), bf16[8,128,512]{2,1,0:T(8,128)(2,1)S(1)}, u32[]{:S(2)}, u32[]{:S(2)}) async-start(bf16[8,128,512]{2,1,0:T(8,128)(2,1)} %bitcast_dynamic-update-slice_fusion), calls=%async_computation | async-start | bytes 2097152 | tf_op jit(solution)/shard_map/all_to_all | solution.py:85
  35.2 1.3 collective-permute-start.2
  37.4 1.9 collective-permute-done.2
  40.5 2.1 gather_fusion.3
  42.6 4.7 %fusion.17 = bf16[8,128,4,120]{1,3,2,0:T(8,128)(2,1)} fusion(f32[120,8,128,4]{2,1,3,0:T(8,128)} %gather_fusion.3, f32[120,8,128,4]{2,1,3,0:T(8,128)S(1)} %gather_fusion.2), kind=kLoop, calls=%fused_computation.36 | loop fusion | flops 983040 | bytes 4915200 | tf_op jit(solution)/shard_map/convert.3
  47.3 16.2 %all-to-all-done = bf16[8,128,512]{2,1,0:T(8,128)(2,1)S(1)} async-done(((bf16[8,128,512]{2,1,0:T(8,128)(2,1)}), bf16[8,128,512]{2,1,0:T(8,128)(2,1)S(1)}, u32[]{:S(2)}, u32[]{:S(2)}) %all-to-all-start) | async-done | bytes 1048608 | tf_op jit(solution)/shard_map/all_to_all | solution.py:85
  64.1 1.3 collective-permute-start
  65.5 1.8 collective-permute-done
  67.9 1.6 fusion.13
  72.2 2.3 fusion.33
  76.3 3.4 all-to-all-start.1
  79.7 7.8 %all-to-all-done.1 = bf16[128,8,64]{0,2,1:T(8,128)(2,1)S(1)} async-done(((bf16[128,8,64]{0,2,1:T(8,128)(2,1)}), bf16[128,8,64]{0,2,1:T(8,128)(2,1)S(1)}, u32[]{:S(2)}, u32[]{:S(2)}) %all-to-all-start.1) | async-done | bytes 131104 | tf_op jit(solution)/shard_map/all_to_all | solution.py:82
  87.6 1.3 collective-permute-start.1
  88.9 6.0 %collective-permute-done.1 = bf16[2,64]{0,1:T(8,128)(2,1)S(1)} collective-permute-done((bf16[2,64]{0,1:T(8,128)(2,1)S(1)}, bf16[2,64]{0,1:T(8,128)(2,1)S(1)}, u32[]{:S(2)}, u32[]{:S(2)}) %collective-permute-start.1) | collective-permute-done | bytes 288 | tf_op jit(solution)/shard_map/ppermute | solution.py:29
  95.3 2.1 gather_fusion
  97.4 2.1 gather_fusion.1
  99.5 2.6 convert_reduce_fusion
  102.2 51.2 %all_gather.9 = f32[64,4,153]{2,1,0:T(4,128)} all-gather(f32[1,4,153]{2,1,0:T(4,128)S(1)} %slice_add_fusion.1), channel_id=1, replica_groups=mesh['seq'=64,'head'=8] {'seq'}, dimensions={0}, use_global_device_ids=true | all-gather | bytes 159120 | tf_op jit(solution)/shard_map/all_gather | solution.py:15
  153.5 3.7 %fusion.16 = bf16[8,128,4,120]{1,3,2,0:T(8,128)(2,1)S(1)} fusion(f32[120,8,128,4]{2,1,3,0:T(8,128)} %gather_fusion.1, f32[120,8,128,4]{2,1,3,0:T(8,128)S(1)} %copy-done.2), kind=kLoop, calls=%fused_computation.35 | loop fusion | flops 983040 | bytes 4915200 | tf_op jit(solution)/shard_map/convert.7
  157.9 1.1 fusion.27
  159.0 1.1 select_reduce_fusion
  160.5 1.9 fusion.12
  162.4 4.7 %fusion.1 = f32[8,4,128,128]{3,2,1,0:T(8,128)} fusion(bf16[8,128,4,153]{1,3,2,0:T(8,128)(2,1)S(1)} %pad_maximum_fusion, f32[8,4,153,128]{3,2,1,0:T(8,128)S(1)} %fusion.33), kind=kOutput, calls=%fused_computation.9 | convolution fusion | flops 842268672 | bytes 5701632 | tf_op jit(solution)/shard_map/nchf,nhfv->nchv/dot_general | solution.py:62
  167.1 17.1 %all-gather.2.cloned.1.call-done = f32[64,4,153,128]{3,1,2,0:T(4,128)} async-done(((f32[1,4,153,128]{3,1,2,0:T(4,128)}), f32[64,4,153,128]{3,1,2,0:T(4,128)}) %all-gather.2.cloned.1.call-update) | async-done | bytes 20054032 | tf_op jit(solution)/shard_map/all_gather | solution.py:15
  184.2 111.9 %while.12 = (s32[]{:T(128)}, f32[4,153,128]{2,1,0:T(8,128)S(1)}, f32[4,153]{1,0:T(4,128)S(1)}, s32[]{:T(128)}, f32[64,4,153,128]{3,1,2,0:T(4,128)}, /*index=5*/f...) while((s32[]{:T(128)}, f32[4,153,128]{2,1,0:T(8,128)S(1)}, f32[4,153]{1,0:T(4,128)S(1)}, s32[]{:T(128)}, ...), condition=%wide.region_4.5_spmd, body=%wide.region_3.4_spmd.sunk | while | flops 78953 | bytes 1574199 | solution.py:23
  184.2 1.1 constant_dynamic-slice_fusion.5
  186.1 1.0 constant_dynamic-slice_fusion.5
  187.9 1.0 constant_dynamic-slice_fusion.5
  189.7 1.0 constant_dynamic-slice_fusion.5
  191.4 1.0 constant_dynamic-slice_fusion.5
  193.2 1.0 constant_dynamic-slice_fusion.5
  195.0 1.0 constant_dynamic-slice_fusion.5
  196.7 1.0 constant_dynamic-slice_fusion.5
  198.5 1.0 constant_dynamic-slice_fusion.5
  200.3 1.0 constant_dynamic-slice_fusion.5
  202.1 1.0 constant_dynamic-slice_fusion.5
  203.8 1.0 constant_dynamic-slice_fusion.5
  205.6 1.0 constant_dynamic-slice_fusion.5
  207.4 1.0 constant_dynamic-slice_fusion.5
  209.1 1.0 constant_dynamic-slice_fusion.5
  210.9 1.0 constant_dynamic-slice_fusion.5
  212.7 1.0 constant_dynamic-slice_fusion.5
  214.5 1.0 constant_dynamic-slice_fusion.5
  216.2 1.0 constant_dynamic-slice_fusion.5
  218.0 1.0 constant_dynamic-slice_fusion.5
  219.8 1.0 constant_dynamic-slice_fusion.5
  221.5 1.0 constant_dynamic-slice_fusion.5
  223.3 1.0 constant_dynamic-slice_fusion.5
  225.1 1.0 constant_dynamic-slice_fusion.5
  226.9 1.0 constant_dynamic-slice_fusion.5
  228.6 1.0 constant_dynamic-slice_fusion.5
  296.7 3.5 %fusion.7 = bf16[8,128,4,128]{1,3,2,0:T(8,128)(2,1)S(1)} fusion(f32[8,4,128,128]{3,2,1,0:T(8,128)} %fusion.12, f32[8,4,128,128]{3,2,1,0:T(8,128)} %fusion.1, bf16[8,128,4,153]{1,3,2,0:T(8,128)(2,1)S(1)} %copy-done.1, f32[8,128,4]{1,2,0:T(4,128)S(1)} %bitcast_add_fusion.2, f32[4,153,128]{2,1,0:T(8,128)S(1)} %get-tuple-element.39), kind=kOutput, calls=%fused_computation.19 | convolution fusion | flops 964689920 | bytes 6825984 | tf_op jit(solution)/shard_map/nchf,hfv->nchv/dot_general | solution.py:141
  300.2 34.3 %all_to_all.62 = bf16[8,128,512]{1,2,0:T(8,128)(2,1)S(1)} all-to-all(bf16[8,128,512]{1,2,0:T(8,128)(2,1)S(1)} %bitcast.124), channel_id=1, replica_groups=mesh['seq'=64,'head'=8] {'head'}, dimensions={0} | all-to-all | bytes 2097152 | tf_op jit(solution)/shard_map/all_to_all | solution.py:158
  334.5 1.3 copy.70
  (226 shorter events, 96.3 us)
Async XLA Ops:
  8.2 19.4 %all-to-all-start.2 = ((bf16[128,8,64]{0,2,1:T(8,128)(2,1)}), bf16[128,8,64]{0,2,1:T(8,128)(2,1)S(1)}, u32[]{:S(2)}, u32[]{:S(2)}) async-start(bf16[128,8,64]{0,2,1:T(8,128)(2,1)} %bitcast.21), calls=%async_computation.2 | async-start | bytes 262144 | tf_op jit(solution)/shard_map/all_to_all | solution.py:83
  15.0 20.0 %copy-start.8 = (s32[120]{0:T(128)S(1)}, s32[120]{0:T(128)}, u32[]{:S(2)}) copy-start(s32[120]{0:T(128)} %constant.72) | copy-start | bytes 1444
  15.0 20.0 %copy-start.9 = (s32[120]{0:T(128)S(1)}, s32[120]{0:T(128)}, u32[]{:S(2)}) copy-start(s32[120]{0:T(128)} %constant.73) | copy-start | bytes 1444
  27.6 35.8 %all-to-all-start = ((bf16[8,128,512]{2,1,0:T(8,128)(2,1)}), bf16[8,128,512]{2,1,0:T(8,128)(2,1)S(1)}, u32[]{:S(2)}, u32[]{:S(2)}) async-start(bf16[8,128,512]{2,1,0:T(8,128)(2,1)} %bitcast_dynamic-update-slice_fusion), calls=%async_computation | async-start | bytes 2097152 | tf_op jit(solution)/shard_map/all_to_all | solution.py:85
  34.2 149.9 %all-gather.2.cloned.1.call-start = ((), (), s32[]{:S(2)}) async-start(), calls=%async_computation.4 | async-start | bytes 20367360 | tf_op jit(solution)/shard_map/all_gather | solution.py:15
  35.2 4.1 %collective-permute-start.2 = (bf16[2,64]{0,1:T(8,128)(2,1)S(1)}, bf16[2,64]{0,1:T(8,128)(2,1)S(1)}, u32[]{:S(2)}, u32[]{:S(2)}) collective-permute-start(bf16[2,64]{0,1:T(8,128)(2,1)S(1)} %slice.126), channel_id=1, source_target_pairs={{0,8},{8,16},{16,24},{24,32},{32,40},{40,48},{48,56},{56,64},{64,7... | collective-permute-start | bytes 776 | tf_op jit(solution)/shard_map/ppermute | solution.py:29
  64.1 3.2 collective-permute-start
  69.6 2.1 copy-start.5
  70.7 1.0 copy-start.3
  72.2 3.3 copy-start.7
  76.3 11.2 %all-to-all-start.1 = ((bf16[128,8,64]{0,2,1:T(8,128)(2,1)}), bf16[128,8,64]{0,2,1:T(8,128)(2,1)S(1)}, u32[]{:S(2)}, u32[]{:S(2)}) async-start(bf16[128,8,64]{0,2,1:T(8,128)(2,1)} %bitcast.15), calls=%async_computation.1 | async-start | bytes 262144 | tf_op jit(solution)/shard_map/all_to_all | solution.py:82
  87.6 7.3 %collective-permute-start.1 = (bf16[2,64]{0,1:T(8,128)(2,1)S(1)}, bf16[2,64]{0,1:T(8,128)(2,1)S(1)}, u32[]{:S(2)}, u32[]{:S(2)}) collective-permute-start(bf16[2,64]{0,1:T(8,128)(2,1)S(1)} %slice.122), channel_id=1, source_target_pairs={{0,8},{8,16},{16,24},{24,32},{32,40},{40,48},{48,56},{56,64},{64,7... | collective-permute-start | bytes 776 | tf_op jit(solution)/shard_map/ppermute | solution.py:29
  99.5 54.0 %copy-start.2 = (f32[120,8,128,4]{2,1,3,0:T(8,128)S(1)}, f32[120,8,128,4]{2,1,3,0:T(8,128)}, u32[]{:S(2)}) copy-start(f32[120,8,128,4]{2,1,3,0:T(8,128)} %gather_fusion) | copy-start | bytes 5898244
  157.3 1.7 copy-start.6
  157.9 4.5 %copy-start = (bf16[8,128,4,153]{1,3,2,0:T(8,128)(2,1)}, bf16[8,128,4,153]{1,3,2,0:T(8,128)(2,1)S(1)}, u32[]{:S(2)}) copy-start(bf16[8,128,4,153]{1,3,2,0:T(8,128)(2,1)S(1)} %pad_maximum_fusion) | copy-start | bytes 3760132
  159.0 1.5 copy-start.4
  184.2 111.9 %copy-start.1 = (bf16[8,128,4,153]{1,3,2,0:T(8,128)(2,1)S(1)}, bf16[8,128,4,153]{1,3,2,0:T(8,128)(2,1)}, u32[]{:S(2)}) copy-start(bf16[8,128,4,153]{1,3,2,0:T(8,128)(2,1)} %copy-done) | copy-start | bytes 3760132
Sparse Core Ops, SparseCore 0:
  75.7 108.4 all-gather.1
